TPU v7x, 32 devices: a whole 2x2x4 slice. The times are simulated.
32 devices in a mesh: groups: 2 (over y), seq: 8 (over z, x), vocab: 2 (over core).
Axes of the slice: x: 2, y: 2, z: 4, core: 2. Of those that a mesh axis runs over, the one named last changes fastest.
Arguments:
- ssm_input: bfloat16 [128, 2560], P(('groups', 'seq'), 'vocab'), parts along dimension 0, may hold values from -6 to 6
- gate_input: bfloat16 [128, 2560], P(('groups', 'seq'), 'vocab'), parts along dimension 0, may hold values from -6 to 6
- b_proj: bfloat16 [128, 128], P(('groups', 'seq')), parts along dimension 0, may hold values from -1.796875 to 1.796875
- readout_matrix: bfloat16 [128, 128], P(('groups', 'seq')), parts along dimension 0, may hold values from -1.796875 to 1.796875
- step_raw: float32 [128, 40], P(('groups', 'seq'), 'vocab'), parts along dimension 0, may hold values from -3 to 7
- step_bias: float32 [40], P('vocab'), may hold values from -1 to 1
- decay_log: float32 [40], P('vocab'), may hold values from -9 to -2
- head_skip_gain: float32 [40], P('vocab'), may hold values from 0.5 to 1.5
- norm_gain: float32 [2560], P('vocab'), may hold values from 0.1 to 1.9
- out_weight: bfloat16 [2560, 2560], P('vocab', 'seq'), may hold values from -0.125 to 0.125
- residual: bfloat16 [128, 2560], P('groups', 'seq'), parts along dimension 0, may hold values from -6 to 6
- final_gain: float32 [2560], replicated, may hold values from 0.1 to 1.9
- head_weight: bfloat16 [2560, 3136], P(None, ('seq', 'vocab')), may hold values from -12.253826 to 12.253826
- mask_table: int32 [96, 3136], P(None, ('seq', 'vocab')), may hold values 0 or 1
- state_ids: int32 [128], P(('groups', 'seq')), parts along dimension 0, may hold values from 0 to 95
- targets: int32 [128], P(('groups', 'seq')), parts along dimension 0, may hold values from 0 to 3135
Outputs:
- token_nll_loss: float32 [128], P(('groups', 'seq', 'vocab')), parts along dimension 0
There are 2 independent parts, one for each index of `groups`. A program takes and returns all parts, laid end to end along the dimension named above; an argument that names none is the same for every part. Nothing has to cross between parts.
All inputs are finite; a program needn't handle non-finite values. No bound on the sum of `mask_table` on one device may be relied on, other than what follows from the above.
Results may differ from a plain program's by a relative error of at most 0.0022.
Values may be sent and summed in bfloat16 or wider, within the bound.
No kernel may reach another device: no remote copies, remote signals or barrier semaphores. Data moves between devices by JAX's collectives and lax.ppermute only.
A program may use at most 192 MiB of HBM per device.

v0:
```python
import jax
import jax.numpy as jnp
from jax import lax
from jax.sharding import PartitionSpec as P


def carried_in(value, axis, join, neutral):
    count, mine = (lax.axis_size(axis), lax.axis_index(axis))
    pieces = jax.tree.map(lambda part: lax.all_gather(part, axis), value)
    total = jax.tree.map(
        lambda part, zero: jnp.full_like(part, 0) + jnp.asarray(zero, part.dtype), value, neutral
    )

    def lap(position, total):
        longer = join(total, jax.tree.map(lambda part: part[position], pieces))
        return jax.tree.map(lambda new, old: jnp.where(position < mine, new, old), longer, total)

    return lax.fori_loop(0, count - 1, lap, total)


def joined(part, axis, combine):
    gathered = jax.tree.map(lambda a: lax.all_gather(a, axis), part)

    def take(source):
        return jax.tree.map(lambda a: lax.dynamic_index_in_dim(a, source, 0, False), gathered)

    return lax.fori_loop(
        1, lax.axis_size(axis), lambda source, state: combine(state, take(source)), take(0)
    )


def carry_join(preceding, later):
    return (preceding[0] * later[0], preceding[1] * later[0][:, None, None] + later[1])


def total_join(first, second):
    top = jnp.maximum(first[0], second[0])
    total = first[1] * jnp.exp(first[0] - top) + second[1] * jnp.exp(second[0] - top)
    return (top, total, first[2] + second[2])


def shards(
    ssm_input,
    gate_input,
    b_proj,
    readout_matrix,
    step_raw,
    step_bias,
    decay_log,
    head_skip_gain,
    norm_gain,
    out_weight,
    residual,
    final_gain,
    head_weight,
    mask_table,
    state_ids,
    targets,
):
    highest = lax.Precision.HIGHEST
    rows = ssm_input.shape[0]
    heads = step_raw.shape[1]
    channels = ssm_input.shape[1]
    head_size = channels // heads
    state_size = b_proj.shape[1]
    step = jax.nn.softplus(step_raw + step_bias[None, :])
    log_rate = step * -jnp.exp(decay_log)[None, :]
    log_cum = jnp.cumsum(log_rate, axis=0)
    values = ssm_input.astype(jnp.float32).reshape(rows, heads, head_size)
    scaled = values * step[:, :, None]
    in_rows = b_proj.astype(jnp.float32)
    out_rows = readout_matrix.astype(jnp.float32)
    correlations = jnp.dot(out_rows, in_rows.T, precision=highest)
    causal = jnp.arange(rows)[:, None] >= jnp.arange(rows)[None, :]
    spread = log_cum[:, None, :] - log_cum[None, :, :]
    weights = jnp.exp(jnp.where(causal[:, :, None], spread, -1e30))
    within = jnp.einsum("tsh,ts,shp->thp", weights, correlations, scaled, precision=highest)
    last_log = log_cum[rows - 1]
    tails = jnp.exp(last_log[None, :] - log_cum)
    local_state = jnp.einsum("sh,shp,sn->hpn", tails, scaled, in_rows, precision=highest)
    identity = (
        jnp.ones((heads,), jnp.float32),
        jnp.zeros((heads, head_size, state_size), jnp.float32),
    )
    _, incoming = carried_in((jnp.exp(last_log), local_state), "seq", carry_join, identity)
    carried = jnp.einsum("th,hpn,tn->thp", jnp.exp(log_cum), incoming, out_rows, precision=highest)
    mixed = within + carried + head_skip_gain[None, :, None] * values
    gated = (mixed.reshape(rows, channels) * jax.nn.silu(gate_input.astype(jnp.float32))).astype(
        jnp.bfloat16
    )
    every_rows, all_states, all_targets = (
        lax.all_gather(gated, "seq", axis=0, tiled=True),
        lax.all_gather(state_ids, "seq", axis=0, tiled=True),
        lax.all_gather(targets, "seq", axis=0, tiled=True),
    )
    every_f = every_rows.astype(jnp.float32)
    squares = lax.psum(jnp.sum(every_f * every_f, axis=-1), "vocab")
    pair_count = lax.axis_size("vocab")
    scale = lax.rsqrt(squares / (channels * pair_count) + 1e-05)
    normed = (every_f * scale[:, None] * norm_gain[None, :]).astype(jnp.bfloat16)
    partial_sum = jnp.dot(normed, out_weight, preferred_element_type=jnp.float32)
    summed = lax.psum(partial_sum, "vocab")
    hidden = (residual.astype(jnp.float32) + summed).astype(jnp.bfloat16)
    full = lax.all_gather(hidden, "seq", axis=1, tiled=True)
    full_f = full.astype(jnp.float32)
    scale_two = lax.rsqrt(jnp.mean(full_f * full_f, axis=-1) + 1e-05)
    final = (full_f * scale_two[:, None] * final_gain[None, :]).astype(jnp.bfloat16)
    vocab_logits = jnp.dot(final, head_weight, preferred_element_type=jnp.float32)
    entries = head_weight.shape[1]
    block_index = lax.axis_index("seq") * pair_count + lax.axis_index("vocab")
    vocab_ids = block_index * entries + jnp.arange(entries, dtype=jnp.int32)
    state_count = mask_table.shape[0]
    one_hot = (all_states[:, None] == jnp.arange(state_count, dtype=jnp.int32)[None, :]).astype(
        jnp.float32
    )
    table_rows = jnp.dot(one_hot, mask_table.astype(jnp.float32))
    is_target = vocab_ids[None, :] == all_targets[:, None]
    allowed = (table_rows > 0.5) | is_target
    local_top = jnp.max(jnp.where(allowed, vocab_logits, -1e30), axis=-1)
    local_total = jnp.sum(
        jnp.where(allowed, jnp.exp(vocab_logits - local_top[:, None]), 0.0), axis=-1
    )
    local_pick = jnp.sum(jnp.where(is_target, vocab_logits, 0.0), axis=-1)
    positions = vocab_logits.shape[0]
    seq_count = lax.axis_size("seq")
    own_rows = positions // (seq_count * pair_count)
    top, total, picked = joined((local_top, local_total, local_pick), ("seq", "vocab"), total_join)
    losses = jnp.log(total) + top - picked
    return lax.dynamic_slice_in_dim(losses, block_index * own_rows, own_rows, 0)


def solution(mesh):
    placed = (
        P(("groups", "seq"), "vocab"),
        P(("groups", "seq"), "vocab"),
        P(("groups", "seq"), None),
        P(("groups", "seq"), None),
        P(("groups", "seq"), "vocab"),
        P("vocab"),
        P("vocab"),
        P("vocab"),
        P("vocab"),
        P("vocab", "seq"),
        P("groups", "seq"),
        P(),
        P(None, ("seq", "vocab")),
        P(None, ("seq", "vocab")),
        P(("groups", "seq")),
        P(("groups", "seq")),
    )
    return jax.shard_map(
        shards, mesh=mesh, in_specs=placed, out_specs=P(("groups", "seq", "vocab")), check_vma=False
    )
```

profile of v0, /device:TPU:0, one launch (start us, length us, event | category | flops | bytes accessed | tf_op | source)
XLA Modules:
  0.0 261.6 jit_solution(14560804017254880365)
XLA Ops:
  6.5 0.7 exponential_negate_fusion
  7.3 0.7 broadcast_multiply_fusion.2
  8.0 0.8 reshape.48
  8.9 0.1 broadcast_multiply_fusion
  9.0 2.3 fusion.23
  11.3 0.1 copy.30
  11.4 0.1 copy.33
  11.5 1.2 dynamic-slice
  12.8 1.3 dynamic-slice.2
  14.7 0.9 dynamic-update-slice.1
  15.5 0.8 dynamic-update-slice
  17.1 13.3 %all-reduce.5 = (s32[64]{0:T(128)S(1)}, s32[64]{0:T(128)S(1)}) all-reduce(s32[64]{0:T(128)S(1)} %dynamic-update-slice.1, s32[64]{0:T(128)S(1)} %dynamic-update-slice), channel_id=1, replica_groups=mesh['groups'=2,'seq'=8,'vocab'=2] {'seq'}, use_global_device_ids=true, to_apply=%add.1 | all-reduce | flops 128 | bytes 1024
  30.3 18.0 %all-gather.4 = f32[8,1,20]{2,1,0:T(1,128)S(1)} all-gather(f32[1,1,20]{2,1,0:T(1,128)S(1)} %get-tuple-element.339), channel_id=1, replica_groups=mesh['groups'=2,'seq'=8,'vocab'=2] {'seq'}, dimensions={0}, use_global_device_ids=true | all-gather | bytes 720 | tf_op jit(solution)/shard_map/all_gather | solution.py:9
  48.3 0.8 fusion.48
  49.2 0.4 convolution_bitcast_fusion.1
  49.5 51.0 %all-gather.8.cloned.1.call-done = f32[160,64,128]{2,1,0:T(8,128)} async-done(((f32[20,64,128]{2,1,0:T(8,128)}), f32[160,64,128]{2,1,0:T(8,128)}) %all-gather.8.cloned.1.call-update) | async-done | bytes 5242896 | tf_op jit(solution)/shard_map/all_gather | solution.py:9
  100.6 9.0 %while.34 = (s32[]{:T(128)}, f32[20,64,128]{2,1,0:T(8,128)S(1)}, s32[]{:T(128)}, f32[8,20]{1,0:T(8,128)S(1)}, f32[8,20,64,128]{3,2,1,0:T(8,128)}, /*index=5*/s32[]{:T(128)}, s32[]{:T(128)}) while((s32[]{:T(128)}, f32[20,64,128]{2,1,0:T(8,128)S(1)}, s32[]{:T(128)}, f32[8,20]{1,0:T(8,128)S(1)}, f32[8,20,64,128]{3,2,1,0:T(8,128)}, ...), condition=%wide.region_2.3_spmd.clone, body=%wide.region_1.2_spmd.clone.sunk | while | flops 655364 | bytes 1966433 | solution.py:18
  100.6 1.3 fusion.57
  101.9 1.2 fusion.57
  103.2 1.2 fusion.57
  104.5 1.2 fusion.57
  105.8 1.2 fusion.57
  107.0 1.2 fusion.57
  108.3 1.2 fusion.57
  109.6 0.9 fusion.10
  110.5 0.1 reshape.46
  110.6 30.6 %all_gather.45 = bf16[64,1280]{1,0:T(8,128)(2,1)S(1)} all-gather(bf16[8,1280]{1,0:T(8,128)(2,1)S(1)} %fusion.40), channel_id=1, replica_groups=mesh['groups'=2,'seq'=8,'vocab'=2] {'seq'}, dimensions={0}, use_global_device_ids=true | all-gather | bytes 184320 | tf_op jit(solution)/shard_map/all_gather | solution.py:92
  141.2 0.1 fusion.12
  141.4 2.5 psum.14
  143.8 1.0 fusion.18
  144.9 16.1 %all-reduce.9.cloned.1.call-done = f32[64,320]{1,0:T(8,128)} async-done(((f32[64,320]{1,0:T(8,128)}), f32[64,320]{1,0:T(8,128)}) %all-reduce.9.cloned.1.call-update) | async-done | bytes 81936 | tf_op jit(solution)/shard_map/psum | solution.py:102
  161.0 0.9 fusion.31
  161.9 31.4 %all-gather.5 = bf16[8,320,64]{1,2,0:T(8,128)(2,1)S(1)} all-gather(bf16[1,320,64]{1,2,0:T(8,128)(2,1)S(1)} %fusion.31), channel_id=1, replica_groups=mesh['groups'=2,'seq'=8,'vocab'=2] {'seq'}, dimensions={0}, use_global_device_ids=true | all-gather | bytes 368640 | tf_op jit(solution)/shard_map/all_gather | solution.py:104
  193.4 0.2 copy.37
  193.6 0.2 reshape.88
  193.8 0.1 multiply_reduce_fusion
  194.0 0.5 fusion.15
  194.5 0.3 select_reduce_fusion.1
  194.7 0.2 fusion.30
  195.0 0.2 dynamic-update-slice.2
  195.2 0.2 dynamic-update-slice.3
  195.4 0.2 dynamic-update-slice.4
  195.6 57.6 %all-reduce.6 = (f32[1024]{0:T(1024)S(1)}, f32[1024]{0:T(1024)S(1)}, f32[1024]{0:T(1024)S(1)}) all-reduce(f32[1024]{0:T(1024)S(1)} %dynamic-update-slice.2, f32[1024]{0:T(1024)S(1)} %dynamic-update-slice.3, f32[1024]{0:T(1024)S(1)} %dynamic-update-slice.4), channel_id=3, replica_groups=mesh['groups'=2,'seq'=8,'vocab'=2] {'seq','vocab'}, use_global_device_ids=true, to_apply=%add.2 | all-reduce | flops 3072 | bytes 24576
  253.3 0.1 reshape.50
  253.3 0.1 reshape.51
  253.4 0.1 reshape.52
  253.5 0.7 while.33
  254.2 0.6 dynamic_slice.60
  (63 shorter events, 0.7 us)
Async XLA Ops:
  6.5 187.4 %copy-start = (bf16[2560,196]{0,1:T(8,128)(2,1)S(1)}, bf16[2560,196]{0,1:T(8,128)(2,1)}, u32[]{:S(2)}) copy-start(bf16[2560,196]{0,1:T(8,128)(2,1)} %param.32) | copy-start | bytes 3010564
  6.5 94.0 %all-gather.8.cloned.1.call-start = ((), (), s32[]{:S(2)}) async-start(), calls=%async_computation.1 | async-start | bytes 5898240 | tf_op jit(solution)/shard_map/all_gather | solution.py:9
  11.3 98.3 %copy-start.6 = (bf16[8,128]{1,0:T(8,128)(2,1)S(1)}, bf16[8,128]{1,0:T(8,128)(2,1)}, u32[]{:S(2)}) copy-start(bf16[8,128]{1,0:T(8,128)(2,1)} %param.23) | copy-start | bytes 6148
  11.3 98.3 %copy-start.7 = (f32[20]{0:T(128)S(1)}, f32[20]{0:T(128)}, u32[]{:S(2)}) copy-start(f32[20]{0:T(128)} %param.27) | copy-start | bytes 244
  11.3 149.7 %all-reduce.9.cloned.1.call-start = ((), (), s32[]{:S(2)}) async-start(), calls=%async_computation | async-start | bytes 196608 | tf_op jit(solution)/shard_map/psum | solution.py:102
  100.6 10.0 %copy-start.3 = (bf16[8,1280]{1,0:T(8,128)(2,1)S(1)}, bf16[8,1280]{1,0:T(8,128)(2,1)}, u32[]{:S(2)}) copy-start(bf16[8,1280]{1,0:T(8,128)(2,1)} %param.21) | copy-start | bytes 61444
  100.6 43.3 %copy-start.1 = (bf16[1280,320]{0,1:T(8,128)(2,1)S(1)}, bf16[1280,320]{0,1:T(8,128)(2,1)}, u32[]{:S(2)}) copy-start(bf16[1280,320]{0,1:T(8,128)(2,1)} %param.29) | copy-start | bytes 2457604
  100.6 43.3 %copy-start.5 = (f32[1280]{0:T(1024)S(1)}, f32[1280]{0:T(1024)}, u32[]{:S(2)}) copy-start(f32[1280]{0:T(1024)} %param.28) | copy-start | bytes 15364
  100.6 60.5 %copy-start.2 = (bf16[64,320]{1,0:T(8,128)(2,1)S(1)}, bf16[64,320]{1,0:T(8,128)(2,1)}, u32[]{:S(2)}) copy-start(bf16[64,320]{1,0:T(8,128)(2,1)} %param.30) | copy-start | bytes 122884
  109.6 84.4 %copy-start.4 = (f32[2560]{0:T(1024)S(1)}, f32[2560]{0:T(1024)}, u32[]{:S(2)}) copy-start(f32[2560]{0:T(1024)} %param.31) | copy-start | bytes 30724
  109.6 84.9 %copy-start.8 = (s32[96,196]{1,0:T(8,128)S(1)}, s32[96,196]{1,0:T(8,128)}, u32[]{:S(2)}) copy-start(s32[96,196]{1,0:T(8,128)} %param.33) | copy-start | bytes 225796
Sparse Core Ops, SparseCore 0:
  11.4 89.1 all-gather.7
  145.0 15.9 all-reduce.8
where the time goes:
time: 262 us
  blocking collectives  153 us (58%)
  waiting for transfers between devices  67.2 us (26%)
  between operations  14.9 us (6%)
  other arithmetic  12.2 us (5%)
  local copies, waits for them, and re-layouts  7.35 us (3%)
  matrix products  6.07 us (2%)
    unnamed x2, blocking collectives  70.9 us
    all_gather x1, waiting for transfers between devices, carried_in(): pieces = jax.tree.map(lambda part: lax.all_gather(part, axis), value)  51 us
    all_gather x1, blocking collectives, shards(): full = lax.all_gather(hidden, 'seq', axis=1, tiled=True)  31.4 us
    all_gather x1, blocking collectives, shards(): lax.all_gather(gated, 'seq', axis=0, tiled=True)  30.6 us
    all_gather x1, blocking collectives, carried_in(): pieces = jax.tree.map(lambda part: lax.all_gather(part, axis), value)  18 us
    psum x1, waiting for transfers between devices, shards(): summed = lax.psum(partial_sum, 'vocab')  16.1 us
    select_n x7, other arithmetic, lap(): jnp.where(position < mine, new, old)  8.7 us
  transfers between devices with their start and end apart: 2, of which 2 were waited for; matrix products, arithmetic and copies ran while one was open for 2% of the time, Pallas kernels for 0%

commit v1 on v0

--- a/solution.py
+++ b/solution.py
@@ -99,7 +99,8 @@
     scale = lax.rsqrt(squares / (channels * pair_count) + 1e-05)
     normed = (every_f * scale[:, None] * norm_gain[None, :]).astype(jnp.bfloat16)
     partial_sum = jnp.dot(normed, out_weight, preferred_element_type=jnp.float32)
-    summed = lax.psum(partial_sum, "vocab")
+    parts = lax.all_gather(partial_sum, "vocab", axis=0, tiled=False)
+    summed = parts.sum(axis=0)
     hidden = (residual.astype(jnp.float32) + summed).astype(jnp.bfloat16)
     full = lax.all_gather(hidden, "seq", axis=1, tiled=True)
     full_f = full.astype(jnp.float32)

time: 262 us -> 246 us (0.939)
  waiting for transfers between devices: 67.2 us -> 51.1 us
    psum x1 -> x0, waiting for transfers between devices: 16.1 us -> none  [shards(): summed = lax.psum(partial_sum, 'vocab')]
  transfers between devices with their start and end apart: 2 -> 1, of which waited for: 2 -> 1; matrix products, arithmetic and copies ran while one was open for 2% -> 2% of each run, Pallas kernels for 0% -> 0%
where the time goes in v1:
time: 246 us; the launch traced here: 245 us
  blocking collectives  155 us (63%)
  waiting for transfers between devices  51.1 us (21%)
  between operations  14.9 us (6%)
  other arithmetic  11.3 us (5%)
  local copies, waits for them, and re-layouts  7.35 us (3%)
  matrix products  5.43 us (2%)
    unnamed x2, blocking collectives  70.9 us
    all_gather x1, waiting for transfers between devices, carried_in(): pieces = jax.tree.map(lambda part: lax.all_gather(part, axis), value)  51.1 us
    all_gather x1, blocking collectives, shards(): full = lax.all_gather(hidden, 'seq', axis=1, tiled=True)  31 us
    all_gather x1, blocking collectives, shards(): lax.all_gather(gated, 'seq', axis=0, tiled=True)  30.6 us
    all_gather x1, blocking collectives, carried_in(): pieces = jax.tree.map(lambda part: lax.all_gather(part, axis), value)  18 us
    select_n x7, other arithmetic, lap(): jnp.where(position < mine, new, old)  8.7 us
    unnamed x31, local copies, waits for them, and re-layouts  4.98 us
  transfers between devices with their start and end apart: 1, of which 1 were waited for; matrix products, arithmetic and copies ran while one was open for 2% of the time, Pallas kernels for 0%

profile of v1, /device:TPU:0, one launch (start us, length us, event | category | flops | bytes accessed | tf_op | source)
XLA Modules:
  0.0 245.5 jit_solution(2076511855801569575)
XLA Ops:
  6.5 0.7 exponential_negate_fusion
  7.3 0.7 broadcast_multiply_fusion.2
  8.0 0.8 reshape.48
  8.9 0.1 broadcast_multiply_fusion
  9.0 2.3 fusion.23
  11.2 0.0 all-gather.9.cloned.1.call-update
  11.3 0.1 copy.30
  11.4 0.1 copy.33
  11.5 1.2 dynamic-slice
  12.7 1.3 dynamic-slice.2
  14.6 0.9 dynamic-update-slice.1
  15.5 0.8 dynamic-update-slice
  17.0 13.3 %all-reduce.5 = (s32[64]{0:T(128)S(1)}, s32[64]{0:T(128)S(1)}) all-reduce(s32[64]{0:T(128)S(1)} %dynamic-update-slice.1, s32[64]{0:T(128)S(1)} %dynamic-update-slice), channel_id=1, replica_groups=mesh['groups'=2,'seq'=8,'vocab'=2] {'seq'}, use_global_device_ids=true, to_apply=%add.1 | all-reduce | flops 128 | bytes 1024
  30.3 18.0 %all-gather.5 = f32[8,1,20]{2,1,0:T(1,128)S(1)} all-gather(f32[1,1,20]{2,1,0:T(1,128)S(1)} %get-tuple-element.339), channel_id=1, replica_groups=mesh['groups'=2,'seq'=8,'vocab'=2] {'seq'}, dimensions={0}, use_global_device_ids=true | all-gather | bytes 720 | tf_op jit(solution)/shard_map/all_gather | solution.py:9
  48.3 0.8 fusion.48
  49.1 0.3 convolution_bitcast_fusion.1
  49.5 51.1 %all-gather.9.cloned.1.call-done = f32[160,64,128]{2,1,0:T(8,128)} async-done(((f32[20,64,128]{2,1,0:T(8,128)}), f32[160,64,128]{2,1,0:T(8,128)}) %all-gather.9.cloned.1.call-update) | async-done | bytes 5242896 | tf_op jit(solution)/shard_map/all_gather | solution.py:9
  100.6 9.0 %while.34 = (s32[]{:T(128)}, f32[20,64,128]{2,1,0:T(8,128)S(1)}, s32[]{:T(128)}, f32[8,20]{1,0:T(8,128)S(1)}, f32[8,20,64,128]{3,2,1,0:T(8,128)}, /*index=5*/s32[]{:T(128)}, s32[]{:T(128)}) while((s32[]{:T(128)}, f32[20,64,128]{2,1,0:T(8,128)S(1)}, s32[]{:T(128)}, f32[8,20]{1,0:T(8,128)S(1)}, f32[8,20,64,128]{3,2,1,0:T(8,128)}, ...), condition=%wide.region_2.3_spmd.clone, body=%wide.region_1.2_spmd.clone.sunk | while | flops 655364 | bytes 1966433 | solution.py:18
  100.6 1.3 fusion.57
  101.9 1.2 fusion.57
  103.2 1.2 fusion.57
  104.5 1.2 fusion.57
  105.8 1.2 fusion.57
  107.0 1.2 fusion.57
  108.3 1.2 fusion.57
  109.6 0.9 fusion.10
  110.5 0.1 reshape.46
  110.6 30.6 %all_gather.51 = bf16[64,1280]{1,0:T(8,128)(2,1)S(1)} all-gather(bf16[8,1280]{1,0:T(8,128)(2,1)S(1)} %fusion.40), channel_id=1, replica_groups=mesh['groups'=2,'seq'=8,'vocab'=2] {'seq'}, dimensions={0}, use_global_device_ids=true | all-gather | bytes 184320 | tf_op jit(solution)/shard_map/all_gather | solution.py:92
  141.2 0.1 fusion.12
  141.4 2.5 %psum.7 = f32[64]{0:T(128)S(1)} all-reduce(f32[64]{0:T(128)S(1)} %fusion.12), channel_id=1, replica_groups=mesh['groups'=2,'seq'=8,'vocab'=2] {'vocab'}, use_global_device_ids=true, to_apply=%region_4.5 | all-reduce | flops 64 | bytes 512 | tf_op jit(solution)/shard_map/psum | solution.py:97
  143.8 0.4 fusion.18
  144.2 1.9 all-gather.1
  146.2 31.0 %all-gather.6 = bf16[8,320,64]{1,2,0:T(8,128)(2,1)S(1)} all-gather(bf16[1,320,64]{1,2,0:T(8,128)(2,1)S(1)} %fusion.31), channel_id=1, replica_groups=mesh['groups'=2,'seq'=8,'vocab'=2] {'seq'}, dimensions={0}, use_global_device_ids=true | all-gather | bytes 368640 | tf_op jit(solution)/shard_map/all_gather | solution.py:105
  177.2 0.2 copy.37
  177.5 0.2 reshape.89
  177.7 0.1 multiply_reduce_fusion
  177.9 0.5 fusion.15
  178.3 0.3 select_reduce_fusion.1
  178.6 0.2 fusion.30
  178.8 0.2 dynamic-update-slice.2
  179.1 0.2 dynamic-update-slice.3
  179.3 0.2 dynamic-update-slice.4
  179.5 57.6 %all-reduce.6 = (f32[1024]{0:T(1024)S(1)}, f32[1024]{0:T(1024)S(1)}, f32[1024]{0:T(1024)S(1)}) all-reduce(f32[1024]{0:T(1024)S(1)} %dynamic-update-slice.2, f32[1024]{0:T(1024)S(1)} %dynamic-update-slice.3, f32[1024]{0:T(1024)S(1)} %dynamic-update-slice.4), channel_id=4, replica_groups=mesh['groups'=2,'seq'=8,'vocab'=2] {'seq','vocab'}, use_global_device_ids=true, to_apply=%add.2 | all-reduce | flops 3072 | bytes 24576
  237.1 0.1 reshape.51
  237.2 0.1 reshape.52
  237.3 0.1 reshape.53
  237.4 0.7 while.33
  238.1 0.6 dynamic_slice.60
  (62 shorter events, 0.7 us)
Async XLA Ops:
  6.5 171.3 %copy-start = (bf16[2560,196]{0,1:T(8,128)(2,1)S(1)}, bf16[2560,196]{0,1:T(8,128)(2,1)}, u32[]{:S(2)}) copy-start(bf16[2560,196]{0,1:T(8,128)(2,1)} %param.32) | copy-start | bytes 3010564
  6.5 94.0 %all-gather.9.cloned.1.call-start = ((), (), s32[]{:S(2)}) async-start(), calls=%async_computation | async-start | bytes 5898240 | tf_op jit(solution)/shard_map/all_gather | solution.py:9
  11.3 98.3 %copy-start.6 = (bf16[8,128]{1,0:T(8,128)(2,1)S(1)}, bf16[8,128]{1,0:T(8,128)(2,1)}, u32[]{:S(2)}) copy-start(bf16[8,128]{1,0:T(8,128)(2,1)} %param.23) | copy-start | bytes 6148
  11.3 98.3 %copy-start.7 = (f32[20]{0:T(128)S(1)}, f32[20]{0:T(128)}, u32[]{:S(2)}) copy-start(f32[20]{0:T(128)} %param.27) | copy-start | bytes 244
  100.6 10.0 %copy-start.3 = (bf16[8,1280]{1,0:T(8,128)(2,1)S(1)}, bf16[8,1280]{1,0:T(8,128)(2,1)}, u32[]{:S(2)}) copy-start(bf16[8,1280]{1,0:T(8,128)(2,1)} %param.21) | copy-start | bytes 61444
  100.6 43.3 %copy-start.1 = (bf16[1280,320]{0,1:T(8,128)(2,1)S(1)}, bf16[1280,320]{0,1:T(8,128)(2,1)}, u32[]{:S(2)}) copy-start(bf16[1280,320]{0,1:T(8,128)(2,1)} %param.29) | copy-start | bytes 2457604
  100.6 43.3 %copy-start.5 = (f32[1280]{0:T(1024)S(1)}, f32[1280]{0:T(1024)}, u32[]{:S(2)}) copy-start(f32[1280]{0:T(1024)} %param.28) | copy-start | bytes 15364
  100.6 45.6 %copy-start.2 = (bf16[64,320]{1,0:T(8,128)(2,1)S(1)}, bf16[64,320]{1,0:T(8,128)(2,1)}, u32[]{:S(2)}) copy-start(bf16[64,320]{1,0:T(8,128)(2,1)} %param.30) | copy-start | bytes 122884
  109.6 68.3 %copy-start.4 = (f32[2560]{0:T(1024)S(1)}, f32[2560]{0:T(1024)}, u32[]{:S(2)}) copy-start(f32[2560]{0:T(1024)} %param.31) | copy-start | bytes 30724
  109.6 68.8 %copy-start.8 = (s32[96,196]{1,0:T(8,128)S(1)}, s32[96,196]{1,0:T(8,128)}, u32[]{:S(2)}) copy-start(s32[96,196]{1,0:T(8,128)} %param.33) | copy-start | bytes 225796
Sparse Core Ops, SparseCore 0:
  11.4 89.1 all-gather.8
